TPU v7x, 256 devices: a whole 4x4x8 slice. The times are simulated.
256 devices in a mesh: seq: 64 (over y, z, core), head: 4 (over x).
Axes of the slice: x: 4, y: 4, z: 8, core: 2. Of those that a mesh axis runs over, the one named last changes fastest.
Arguments:
- signal: bfloat16 [16384, 2048], P('seq', 'head'), may hold values from -6 to 6
- gate: bfloat16 [16384, 2048], P('seq', 'head'), may hold values from -6 to 6
- skip: float32 [2048], P('head'), may hold values from -4 to 4
- w_first: float32 [33, 64], replicated, may hold values from -1 to 1
- b_first: float32 [64], replicated, may hold values from -3.140625 to 3.140625
- freq: float32 [64], replicated, may hold values from 0.5 to 2
- w_mid: float32 [64, 64], replicated, may hold values from -0.75 to 0.75
- w_last: float32 [64, 2048], P(None, 'head'), may hold values from -0.046875 to 0.046875
- rate: float32 [2048], P('head'), may hold values from 0.00014648438 to 0.08
- out_w: bfloat16 [2048, 2048], P('head'), may hold values from -0.125 to 0.125
Outputs:
- output: bfloat16 [16384, 2048], P('seq', 'head')
All inputs are finite; a program needn't handle non-finite values.
Results may differ from a plain program's by a relative error of at most 0.0054.
Values may be sent and summed in bfloat16 or wider, within the bound.
A program may use at most 64 MiB of HBM per device.

v0:
```python
import math

import jax
import jax.numpy as jnp
from jax import lax
from jax.sharding import PartitionSpec as P

K = 2048
BANDS = 16


def shifted(x, axis, by):
    size = lax.axis_size(axis)
    pairs = [(i, i + by) for i in range(size) if 0 <= i + by < size]
    return lax.ppermute(x, axis, pairs)


def in_blocks_2(x, dim, size):
    dims = x.shape
    tiles = x.reshape(*dims[:dim], size, dims[dim] // size, *dims[dim + 1 :])
    return jnp.moveaxis(tiles, dim, 0)


def sum_at_owner(x, axis, dim):
    size = lax.axis_size(axis)
    tiles = lax.all_to_all(in_blocks_2(x, dim, size), axis, 0, 0, tiled=True)
    return jnp.sum(tiles, axis=0)


def make_filter(w_first, b_first, freq, w_mid, w_last, rate, count):
    highest = lax.Precision.HIGHEST
    position = jnp.arange(count).astype(jnp.float32)
    bands = jnp.arange(1, BANDS + 1).astype(jnp.float32)
    angles = 2.0 * math.pi * position[:, None] * bands[None, :] / K
    features = jnp.concatenate([position[:, None] / K, jnp.cos(angles), jnp.sin(angles)], 1)
    first = jnp.sin(freq * (jnp.dot(features, w_first, precision=highest) + b_first))
    second = jnp.sin(freq * jnp.dot(first, w_mid, precision=highest))
    raw = jnp.dot(second, w_last, precision=highest)
    return (raw * jnp.exp(-rate[None, :] * position[:, None])).astype(jnp.bfloat16)


def transform_tables(block):
    doubled = 2 * block
    taps = jnp.arange(block)
    freqs = jnp.arange(block)
    outputs = jnp.arange(doubled)
    scale_angle = 2.0 * math.pi / doubled
    phase = (freqs[:, None] * taps[None, :] % doubled).astype(jnp.float32) * scale_angle
    alternate = (1 - 2 * (taps % 2)).astype(jnp.float32)
    forward_real = jnp.cos(phase)
    forward_imag = jnp.where(freqs[:, None] == 0, alternate[None, :], -jnp.sin(phase))
    phase_back = (outputs[:, None] * freqs[None, :] % doubled).astype(jnp.float32) * scale_angle
    alternate_back = (1 - 2 * (outputs % 2)).astype(jnp.float32)
    weights = jnp.where(freqs == 0, 1.0, 2.0).astype(jnp.float32)
    back_real = weights[None, :] * jnp.cos(phase_back) / doubled
    back_imag = (
        jnp.where(freqs[None, :] == 0, alternate_back[:, None], -2.0 * jnp.sin(phase_back))
        / doubled
    )
    return (forward_real, forward_imag, back_real, back_imag)


def long_convolve(padded, filt, length_local):
    highest = lax.Precision.HIGHEST
    channels = padded.shape[1]
    block = min(128, length_local)
    segments = K // block
    out_blocks = length_local // block
    in_blocks = padded.shape[0] // block
    forward_real, forward_imag, back_real, back_imag = transform_tables(block)
    values = padded.astype(jnp.float32).reshape(in_blocks, block, channels)
    kernels = filt.astype(jnp.float32).reshape(segments, block, channels)[::-1]
    spec_real = jnp.einsum("ft,ntc->nfc", forward_real, values, precision=highest)
    spec_imag = jnp.einsum("ft,ntc->nfc", forward_imag, values, precision=highest)
    kern_real = jnp.einsum("ft,ntc->nfc", forward_real, kernels, precision=highest)
    kern_imag = jnp.einsum("ft,ntc->nfc", forward_imag, kernels, precision=highest)
    upper = (jnp.arange(block) >= 1).astype(jnp.float32)[:, None]
    sums_real = []
    sums_imag = []
    for index in range(out_blocks + 1):
        window_real = spec_real[index : index + segments]
        window_imag = spec_imag[index : index + segments]
        both_imag = kern_imag * window_imag
        sums_real.append(jnp.sum(kern_real * window_real - upper * both_imag, 0))
        cross = kern_real * window_imag + kern_imag * window_real
        sums_imag.append(jnp.sum(upper * cross + (1.0 - upper) * both_imag, 0))
    total_real = jnp.stack(sums_real, 0)
    total_imag = jnp.stack(sums_imag, 0)
    pieces = jnp.einsum("tf,kfc->ktc", back_real, total_real, precision=highest)
    pieces = pieces + jnp.einsum("tf,kfc->ktc", back_imag, total_imag, precision=highest)
    joined = pieces[1:, :block] + pieces[:-1, block:]
    return joined.reshape(length_local, channels)


def local(signal, gate, skip, w_first, b_first, freq, w_mid, w_last, rate, out_w):
    length_local, channels = signal.shape
    filt = make_filter(w_first, b_first, freq, w_mid, w_last, rate, K)
    reach = K // length_local
    earlier = [shifted(signal, "seq", step) for step in range(reach, 0, -1)]
    padded = jnp.concatenate(earlier + [signal], 0)
    conv = long_convolve(padded, filt, length_local)
    mixed = (gate.astype(jnp.float32) * (conv + skip[None, :] * signal.astype(jnp.float32))).astype(
        jnp.bfloat16
    )
    terms = jnp.dot(mixed, out_w, preferred_element_type=jnp.float32)
    result = sum_at_owner(terms, "head", 1)
    return result.astype(jnp.bfloat16)


def solution(mesh):
    placed = (
        P("seq", "head"),
        P("seq", "head"),
        P("head"),
        P(),
        P(),
        P(),
        P(),
        P(None, "head"),
        P("head"),
        P("head", None),
    )
    return jax.shard_map(
        local, mesh=mesh, in_specs=placed, out_specs=P("seq", "head"), check_vma=False
    )
```

profile of v0, /device:TPU:2, one launch (start us, length us, event | category | flops | bytes accessed | tf_op | source)
XLA Modules:
  0.0 159.7 jit_solution(65257332225828398)
XLA Ops:
  0.0 9.9 %collective-permute-start = (bf16[256,512]{1,0:T(8,128)(2,1)}, bf16[256,512]{1,0:T(8,128)(2,1)}, u32[]{:S(2)}, u32[]{:S(2)}) collective-permute-start(bf16[256,512]{1,0:T(8,128)(2,1)} %param.10), channel_id=1, source_target_pairs={{0,32},{4,36},{8,40},{12,44},{16,48},{20,52},{24,56},{28,60},{32,6... | collective-permute-start | bytes 786440 | tf_op jit(solution)/shard_map/ppermute | solution.py:15
  9.9 3.7 %collective-permute-start.1 = (bf16[256,512]{1,0:T(8,128)(2,1)}, bf16[256,512]{1,0:T(8,128)(2,1)}, u32[]{:S(2)}, u32[]{:S(2)}) collective-permute-start(bf16[256,512]{1,0:T(8,128)(2,1)} %param.10), channel_id=1, source_target_pairs={{0,28},{4,32},{8,36},{12,40},{16,44},{20,48},{24,52},{28,56},{32,6... | collective-permute-start | bytes 786440 | tf_op jit(solution)/shard_map/ppermute | solution.py:15
  13.6 2.3 %collective-permute-start.2 = (bf16[256,512]{1,0:T(8,128)(2,1)}, bf16[256,512]{1,0:T(8,128)(2,1)S(1)}, u32[]{:S(2)}, u32[]{:S(2)}) collective-permute-start(bf16[256,512]{1,0:T(8,128)(2,1)} %param.10), channel_id=1, source_target_pairs={{0,24},{4,28},{8,32},{12,36},{16,40},{20,44},{24,48},{28,52},{32,5... | collective-permute-start | bytes 786440 | tf_op jit(solution)/shard_map/ppermute | solution.py:15
  16.0 6.5 %collective-permute-start.3 = (bf16[256,512]{1,0:T(8,128)(2,1)}, bf16[256,512]{1,0:T(8,128)(2,1)S(1)}, u32[]{:S(2)}, u32[]{:S(2)}) collective-permute-start(bf16[256,512]{1,0:T(8,128)(2,1)} %param.10), channel_id=1, source_target_pairs={{0,20},{4,24},{8,28},{12,32},{16,36},{20,40},{24,44},{28,48},{32,5... | collective-permute-start | bytes 786440 | tf_op jit(solution)/shard_map/ppermute | solution.py:15
  22.4 3.4 %collective-permute-start.4 = (bf16[256,512]{1,0:T(8,128)(2,1)}, bf16[256,512]{1,0:T(8,128)(2,1)S(1)}, u32[]{:S(2)}, u32[]{:S(2)}) collective-permute-start(bf16[256,512]{1,0:T(8,128)(2,1)} %param.10), channel_id=1, source_target_pairs={{0,16},{4,20},{8,24},{12,28},{16,32},{20,36},{24,40},{28,44},{32,4... | collective-permute-start | bytes 786440 | tf_op jit(solution)/shard_map/ppermute | solution.py:15
  27.1 3.1 %fusion.19 = f32[2048,64]{0,1:T(8,128)S(1)} fusion(f32[33,64]{1,0:T(8,128)} %param.13, f32[2048,16]{0,1:T(8,128)S(1)} %get-tuple-element.12, f32[2048,16]{0,1:T(8,128)S(1)} %get-tuple-element.11, f32[2048,1]{0,1:T(1,128)S(1)} %convert_multiply_fusion, f32[64]{0:T(128)} %param.14, f32[64]{0:T(128)} %param.15), kind=kOutput, calls=%fused_computation.34 | convolution fusion | flops 52301824 | bytes 803584 | tf_op jit(solution)/shard_map/dot_general | solution.py:36
  30.2 3.0 %fusion.20 = f32[2048,64]{0,1:T(8,128)S(1)} fusion(f32[2048,64]{0,1:T(8,128)S(1)} %fusion.19, f32[64,64]{1,0:T(8,128)} %param.16, f32[64]{0:T(128)} %param.15), kind=kOutput, calls=%fused_computation.35 | convolution fusion | flops 100794368 | bytes 1065216 | tf_op jit(solution)/shard_map/dot_general | solution.py:37
  33.2 5.9 %multiply_convert_fusion = bf16[2048,512]{1,0:T(8,128)(2,1)} fusion(f32[2048,64]{0,1:T(8,128)S(1)} %fusion.20, f32[64,512]{1,0:T(8,128)} %param.17, f32[2048]{0:T(1024)S(1)} %iota_convert_fusion, f32[512]{0:T(512)S(1)} %neg.9), kind=kOutput, calls=%fused_computation.30 | convolution fusion | flops 808452096 | bytes 2762752 | tf_op jit(solution)/shard_map/dot_general | solution.py:38
  39.2 4.1 %copy.15 = f32[16,128,512]{1,2,0:T(8,128)} copy(bf16[16,128,512]{2,1,0:T(8,128)(2,1)} %bitcast.129) | data formatting | bytes 6291456 | tf_op jit(solution)/shard_map/reshape | solution.py:72
  43.2 4.6 %rev.3 = f32[16,128,512]{1,2,0:T(8,128)} reverse(f32[16,128,512]{1,2,0:T(8,128)} %copy.15), dimensions={0} | reverse | bytes 8388608 | tf_op jit(solution)/shard_map/rev | solution.py:72
  47.8 7.1 %fusion.63 = f32[16,512,128]{2,1,0:T(8,128)} fusion(f32[16,128,512]{1,2,0:T(8,128)} %rev.3), kind=kOutput, calls=%fused_computation.91 | convolution fusion | flops 1610842112 | bytes 8388608 | tf_op jit(solution)/shard_map/ft,ntc->nfc/dot_general | solution.py:75
  54.9 1.3 collective-permute-start.5
  56.2 1.0 constant_dynamic-update-slice_fusion.8
  57.2 2.8 %collective-permute-start.6 = (bf16[256,512]{1,0:T(8,128)(2,1)S(1)}, bf16[256,512]{1,0:T(8,128)(2,1)S(1)}, u32[]{:S(2)}, u32[]{:S(2)}) collective-permute-start(bf16[256,512]{1,0:T(8,128)(2,1)S(1)} %copy-done.2), channel_id=1, source_target_pairs={{0,8},{4,12},{8,16},{12,20},{16,24},{20,28},{24,32},{28,36},{32,40... | collective-permute-start | bytes 786440 | tf_op jit(solution)/shard_map/ppermute | solution.py:15
  60.0 1.0 constant_dynamic-update-slice_fusion.7
  61.0 3.3 %collective-permute-start.7 = (bf16[256,512]{1,0:T(8,128)(2,1)S(1)}, bf16[256,512]{1,0:T(8,128)(2,1)S(1)}, u32[]{:S(2)}, u32[]{:S(2)}) collective-permute-start(bf16[256,512]{1,0:T(8,128)(2,1)S(1)} %copy-done.2), channel_id=1, source_target_pairs={{0,4},{4,8},{8,12},{12,16},{16,20},{20,24},{24,28},{28,32},{32,36}... | collective-permute-start | bytes 786440 | tf_op jit(solution)/shard_map/ppermute | solution.py:15
  64.4 9.7 %collective-permute-done.4 = bf16[256,512]{1,0:T(8,128)(2,1)S(1)} collective-permute-done((bf16[256,512]{1,0:T(8,128)(2,1)}, bf16[256,512]{1,0:T(8,128)(2,1)S(1)}, u32[]{:S(2)}, u32[]{:S(2)}) %collective-permute-start.4) | collective-permute-done | bytes 262176 | tf_op jit(solution)/shard_map/ppermute | solution.py:15
  74.1 12.3 %collective-permute-done.5 = bf16[256,512]{1,0:T(8,128)(2,1)S(1)} collective-permute-done((bf16[256,512]{1,0:T(8,128)(2,1)S(1)}, bf16[256,512]{1,0:T(8,128)(2,1)S(1)}, u32[]{:S(2)}, u32[]{:S(2)}) %collective-permute-start.5) | collective-permute-done | bytes 262176 | tf_op jit(solution)/shard_map/ppermute | solution.py:15
  86.4 5.6 %collective-permute-done.6 = bf16[256,512]{1,0:T(8,128)(2,1)S(1)} collective-permute-done((bf16[256,512]{1,0:T(8,128)(2,1)S(1)}, bf16[256,512]{1,0:T(8,128)(2,1)S(1)}, u32[]{:S(2)}, u32[]{:S(2)}) %collective-permute-start.6) | collective-permute-done | bytes 262176 | tf_op jit(solution)/shard_map/ppermute | solution.py:15
  92.1 3.0 %convolution_bitcast_fusion.1 = f32[18,128,512]{1,2,0:T(8,128)S(1)} fusion(bf16[18,128,512]{2,1,0:T(8,128)(2,1)S(1)} %bitcast.125), kind=kOutput, calls=%fused_computation.37 | convolution fusion | flops 1812168704 | bytes 7077888 | tf_op jit(solution)/shard_map/ft,ntc->nfc/dot_general | solution.py:73
  95.1 3.0 %convolution_bitcast_fusion = f32[18,128,512]{1,2,0:T(8,128)S(1)} fusion(bf16[18,128,512]{2,1,0:T(8,128)(2,1)S(1)} %bitcast.126, f32[128]{0:T(128)S(1)} %fusion.90, pred[128]{0:T(512)(128)(4,1)S(1)} %get-tuple-element.14), kind=kOutput, calls=%fused_computation.36 | convolution fusion | flops 1812201472 | bytes 7078528 | tf_op jit(solution)/shard_map/ft,ntc->nfc/dot_general | solution.py:74
  98.2 12.8 %fusion.3 = (f32[128,512]{0,1:T(8,128)}, f32[128,512]{0,1:T(8,128)}, f32[128,512]{0,1:T(8,128)}, f32[128,512]{0,1:T(8,128)}, f32[128,512]{0,1:T(8,128)}, /*index=5*/f32[128,512]{0,1:T(8,128)}) fusion(f32[16,512,128]{2,1,0:T(8,128)} %fusion.63, f32[18,128,512]{1,2,0:T(8,128)S(1)} %convolution_bitcast_fusion, ...), kind=kOutput, calls=%fused_computation.9 | convolution fusion | flops 1648230400 | bytes 35128960 | tf_op jit(solution)/shard_map/ft,ntc->nfc/dot_general | solution.py:76
  110.9 1.1 copy.20
  112.0 1.1 copy.18
  113.1 1.8 %copy.19 = f32[128,512]{1,0:T(8,128)} copy(f32[128,512]{0,1:T(8,128)} %get-tuple-element.8) | data formatting | bytes 524288 | tf_op jit(solution)/shard_map/reduce_sum | solution.py:84
  114.9 1.1 copy.21
  116.0 1.8 %copy.22 = f32[128,512]{1,0:T(8,128)} copy(f32[128,512]{0,1:T(8,128)} %get-tuple-element.6) | data formatting | bytes 524288 | tf_op jit(solution)/shard_map/reduce_sum | solution.py:86
  117.8 1.8 %copy.23 = f32[128,512]{1,0:T(8,128)} copy(f32[128,512]{0,1:T(8,128)} %get-tuple-element.7) | data formatting | bytes 524288 | tf_op jit(solution)/shard_map/reduce_sum | solution.py:86
  119.6 2.9 %fusion.21 = f32[3,512,256]{1,2,0:T(8,128)S(1)} fusion(f32[1,128,512]{2,1,0:T(8,128)S(1)} %bitcast.130, f32[1,128,512]{2,1,0:T(8,128)} %bitcast.134, f32[1,128,512]{2,1,0:T(8,128)S(1)} %bitcast.132, f32[128]{0:T(128)S(1)} %broadcast_select_fusion), kind=kOutput, calls=%fused_computation.40 | convolution fusion | flops 604897280 | bytes 2359808 | tf_op jit(solution)/shard_map/tf,kfc->ktc/dot_general | solution.py:89
  122.5 3.0 %add_bitcast_fusion = f32[3,256,512]{2,1,0:T(8,128)S(1)} fusion(f32[3,512,256]{1,2,0:T(8,128)S(1)} %fusion.21, f32[1,128,512]{2,1,0:T(8,128)} %bitcast.135, f32[1,128,512]{2,1,0:T(8,128)} %bitcast.133, f32[1,128,512]{2,1,0:T(8,128)S(1)} %bitcast.131, f32[256]{0:T(256)S(1)} %fusion.87, pred[128]{0:T(512)(128)(4,1)S(1)} %get-tuple-element.14), kind=kOutput, calls=%fused_computation.39 | convolution fusion | flops 605323264 | bytes 3933312 | tf_op jit(solution)/shard_map/tf,kfc->ktc/dot_general | solution.py:90
  126.7 30.4 %all_to_all.5 = f32[4,256,512]{2,1,0:T(8,128)} all-to-all(f32[4,256,512]{2,1,0:T(8,128)S(1)} %bitcast.128), channel_id=1, replica_groups=mesh['seq'=64,'head'=4] {'head'}, dimensions={0} | all-to-all | bytes 4194304 | tf_op jit(solution)/shard_map/all_to_all | solution.py:26
  157.1 2.6 %reduce_sum.69 = bf16[256,512]{1,0:T(8,128)(2,1)} reduce(f32[4,256,512]{2,1,0:T(8,128)} %all_to_all.5, f32[]{:T(128)} %constant.73.clone.1), dimensions={0}, to_apply=%region_6.7 | reduce | flops 393216 | bytes 2359300 | tf_op jit(solution)/shard_map/reduce_sum | solution.py:27
  (37 shorter events, 2.6 us)
Async XLA Ops:
  0.0 125.7 %copy-start = (bf16[512,2048]{1,0:T(8,128)(2,1)S(1)}, bf16[512,2048]{1,0:T(8,128)(2,1)}, u32[]{:S(2)}) copy-start(bf16[512,2048]{1,0:T(8,128)(2,1)} %param.19) | copy-start | bytes 6291460
  0.0 54.9 %collective-permute-start = (bf16[256,512]{1,0:T(8,128)(2,1)}, bf16[256,512]{1,0:T(8,128)(2,1)}, u32[]{:S(2)}, u32[]{:S(2)}) collective-permute-start(bf16[256,512]{1,0:T(8,128)(2,1)} %param.10), channel_id=1, source_target_pairs={{0,32},{4,36},{8,40},{12,44},{16,48},{20,52},{24,56},{28,60},{32,6... | collective-permute-start | bytes 786440 | tf_op jit(solution)/shard_map/ppermute | solution.py:15
  9.9 47.3 %collective-permute-start.1 = (bf16[256,512]{1,0:T(8,128)(2,1)}, bf16[256,512]{1,0:T(8,128)(2,1)}, u32[]{:S(2)}, u32[]{:S(2)}) collective-permute-start(bf16[256,512]{1,0:T(8,128)(2,1)} %param.10), channel_id=1, source_target_pairs={{0,28},{4,32},{8,36},{12,40},{16,44},{20,48},{24,52},{28,56},{32,6... | collective-permute-start | bytes 786440 | tf_op jit(solution)/shard_map/ppermute | solution.py:15
  13.6 47.4 %collective-permute-start.2 = (bf16[256,512]{1,0:T(8,128)(2,1)}, bf16[256,512]{1,0:T(8,128)(2,1)S(1)}, u32[]{:S(2)}, u32[]{:S(2)}) collective-permute-start(bf16[256,512]{1,0:T(8,128)(2,1)} %param.10), channel_id=1, source_target_pairs={{0,24},{4,28},{8,32},{12,36},{16,40},{20,44},{24,48},{28,52},{32,5... | collective-permute-start | bytes 786440 | tf_op jit(solution)/shard_map/ppermute | solution.py:15
  16.0 48.4 %collective-permute-start.3 = (bf16[256,512]{1,0:T(8,128)(2,1)}, bf16[256,512]{1,0:T(8,128)(2,1)S(1)}, u32[]{:S(2)}, u32[]{:S(2)}) collective-permute-start(bf16[256,512]{1,0:T(8,128)(2,1)} %param.10), channel_id=1, source_target_pairs={{0,20},{4,24},{8,28},{12,32},{16,36},{20,40},{24,44},{28,48},{32,5... | collective-permute-start | bytes 786440 | tf_op jit(solution)/shard_map/ppermute | solution.py:15
  22.4 51.6 %collective-permute-start.4 = (bf16[256,512]{1,0:T(8,128)(2,1)}, bf16[256,512]{1,0:T(8,128)(2,1)S(1)}, u32[]{:S(2)}, u32[]{:S(2)}) collective-permute-start(bf16[256,512]{1,0:T(8,128)(2,1)} %param.10), channel_id=1, source_target_pairs={{0,16},{4,20},{8,24},{12,28},{16,32},{20,36},{24,40},{28,44},{32,4... | collective-permute-start | bytes 786440 | tf_op jit(solution)/shard_map/ppermute | solution.py:15
  47.8 7.1 %copy-start.2 = (bf16[256,512]{1,0:T(8,128)(2,1)S(1)}, bf16[256,512]{1,0:T(8,128)(2,1)}, u32[]{:S(2)}) copy-start(bf16[256,512]{1,0:T(8,128)(2,1)} %param.10) | copy-start | bytes 786436
  54.9 31.5 %collective-permute-start.5 = (bf16[256,512]{1,0:T(8,128)(2,1)S(1)}, bf16[256,512]{1,0:T(8,128)(2,1)S(1)}, u32[]{:S(2)}, u32[]{:S(2)}) collective-permute-start(bf16[256,512]{1,0:T(8,128)(2,1)S(1)} %copy-done.2), channel_id=1, source_target_pairs={{0,12},{4,16},{8,20},{12,24},{16,28},{20,32},{24,36},{28,40},{32,4... | collective-permute-start | bytes 786440 | tf_op jit(solution)/shard_map/ppermute | solution.py:15
  57.2 34.8 %collective-permute-start.6 = (bf16[256,512]{1,0:T(8,128)(2,1)S(1)}, bf16[256,512]{1,0:T(8,128)(2,1)S(1)}, u32[]{:S(2)}, u32[]{:S(2)}) collective-permute-start(bf16[256,512]{1,0:T(8,128)(2,1)S(1)} %copy-done.2), channel_id=1, source_target_pairs={{0,8},{4,12},{8,16},{12,20},{16,24},{20,28},{24,32},{28,36},{32,40... | collective-permute-start | bytes 786440 | tf_op jit(solution)/shard_map/ppermute | solution.py:15
  61.0 31.0 %collective-permute-start.7 = (bf16[256,512]{1,0:T(8,128)(2,1)S(1)}, bf16[256,512]{1,0:T(8,128)(2,1)S(1)}, u32[]{:S(2)}, u32[]{:S(2)}) collective-permute-start(bf16[256,512]{1,0:T(8,128)(2,1)S(1)} %copy-done.2), channel_id=1, source_target_pairs={{0,4},{4,8},{8,12},{12,16},{16,20},{20,24},{24,28},{28,32},{32,36}... | collective-permute-start | bytes 786440 | tf_op jit(solution)/shard_map/ppermute | solution.py:15
  95.1 3.1 %copy-start.1 = (f32[16,128,512]{1,2,0:T(8,128)S(1)}, f32[16,128,512]{1,2,0:T(8,128)}, u32[]{:S(2)}) copy-start(f32[16,128,512]{1,2,0:T(8,128)} %rev.3) | copy-start | bytes 12582916
  117.8 7.8 %copy-start.4 = (f32[512]{0:T(512)S(1)}, f32[512]{0:T(512)}, u32[]{:S(2)}) copy-start(f32[512]{0:T(512)} %param.12) | copy-start | bytes 6148
  119.6 6.0 %copy-start.3 = (bf16[256,512]{1,0:T(8,128)(2,1)S(1)}, bf16[256,512]{1,0:T(8,128)(2,1)}, u32[]{:S(2)}) copy-start(bf16[256,512]{1,0:T(8,128)(2,1)} %param.11) | copy-start | bytes 786436
where the time goes:
time: 163 us; the launch traced here: 160 us
  matrix products  44.5 us (27%)
  starting transfers between devices  33.2 us (20%)
  blocking collectives  30.4 us (19%)
  waiting for transfers between devices  27.6 us (17%)
  local copies, waits for them, and re-layouts  19.5 us (12%)
  other arithmetic  4.07 us (2%)
    ppermute x8, starting transfers between devices, shifted(): return lax.ppermute(x, axis, pairs)  33.2 us
    all_to_all x1, blocking collectives, sum_at_owner(): tiles = lax.all_to_all(in_blocks_2(x, dim, size), axis, 0, 0, tiled=True)  30.4 us
    ppermute x8, waiting for transfers between devices, shifted(): return lax.ppermute(x, axis, pairs)  27.6 us
    dot_general x1, matrix products, long_convolve(): jnp.einsum('ft,ntc->nfc', forward_imag, kernels, precision=highest)  12.8 us
    dot_general x1, matrix products, long_convolve(): jnp.einsum('ft,ntc->nfc', forward_real, kernels, precision=highest)  7.05 us
    dot_general x1, matrix products, make_filter(): raw = jnp.dot(second, w_last, precision=highest)  5.92 us
    reduce_sum x3, local copies, waits for them, and re-layouts, long_convolve(): sums_imag.append(jnp.sum(upper * cross + (1.0 - upper) * both_imag, 0))  4.66 us
    rev x1, local copies, waits for them, and re-layouts, long_convolve(): kernels = filt.astype(jnp.float32).reshape(segments, block, channels)[::-1]  4.56 us
  transfers between devices with their start and end apart: 8, of which 3 were waited for; matrix products, arithmetic and copies ran while one was open for 19% of the time, Pallas kernels for 0%

commit v1 on v0

v1 whole, which is shorter than its diff:
```python
import functools
import math

import jax
import jax.numpy as jnp
import numpy as np
from jax import lax
from jax.experimental import pallas as pl
from jax.experimental.pallas import tpu as pltpu
from jax.sharding import PartitionSpec as P

K = 2048
BANDS = 16
LANES = 128
MESH = pl.DeviceIdType.MESH


def features():
    t = np.arange(K, dtype=np.float64)
    bands = np.arange(1, BANDS + 1, dtype=np.float64)
    angles = 2.0 * math.pi * t[None, :] * bands[:, None] / K
    rows = np.concatenate([t[None] / K, np.cos(angles), np.sin(angles), np.ones((1, K))], 0)
    rows = np.concatenate([rows, np.zeros((40 - rows.shape[0], K))], 0)
    return rows.astype(np.float32)


def sine(x):
    turns = jnp.round(x * (1.0 / math.pi))
    r = (x - turns * 3.140625) - turns * (math.pi - 3.140625)
    s = r * r
    p = -1.0 / 39916800.0
    for c in (1.0 / 362880.0, -1.0 / 5040.0, 1.0 / 120.0, -1.0 / 6.0):
        p = p * s + c
    v = r + r * s * p
    odd = jnp.bitwise_and(turns.astype(jnp.int32), 1)
    return jnp.where(odd == 1, -v, v)


def rows_of(tile, count):
    copies = jnp.broadcast_to(tile[None], (count // tile.shape[0], *tile.shape))
    return copies.reshape(count, tile.shape[1])


def dot_t(a, b):
    return lax.dot_general(
        a, b, (((0,), (0,)), ((), ())),
        precision=lax.Precision.HIGHEST, preferred_element_type=jnp.float32,
    )


def kernel(
    n, heads, sig_hbm, gate_hbm, skip_ref, wf_ref, bf_ref, freq_ref, wm_ref, wl_ref, rate_ref, w_hbm, feat_ref,
    out_ref,
    sig, gate, w, xsend, xrecv, xf, params, h_ref, skips, toep, yf, ysend, yrecv, mixed, part, psend, precv,
    in_sems, xs_sem, xr_sem, ys_sem, yr_sem, ps_sems, pr_sems,
):
    me = lax.axis_index("seq")
    hd = lax.axis_index("head")
    group = xsend.shape[1] // 2
    rows = sig.shape[0]
    width = sig.shape[1]

    loads = [
        pltpu.make_async_copy(sig_hbm, sig, in_sems.at[0]),
        pltpu.make_async_copy(gate_hbm, gate, in_sems.at[1]),
        pltpu.make_async_copy(w_hbm, w, in_sems.at[2]),
    ]
    for c in loads:
        c.start()

    barrier = pltpu.get_barrier_semaphore()

    def greet(k, carry):
        pl.semaphore_signal(barrier, inc=1, device_id={"seq": lax.rem(me + k, n)}, device_id_type=MESH)
        return carry

    lax.fori_loop(1, n, greet, 0)
    for k in range(1, heads):
        pl.semaphore_signal(barrier, inc=1, device_id={"head": lax.rem(hd + k, heads)}, device_id_type=MESH)

    loads[0].wait()
    xt = sig[...].astype(jnp.float32).T.reshape(n, group, rows)
    xsend[...] = jnp.concatenate([xt[:, :, :LANES], xt[:, :, LANES:]], 1).astype(jnp.bfloat16)

    pl.semaphore_wait(barrier, n - 1 + heads - 1)

    def send_x(k, carry):
        to = lax.rem(me + k, n)
        pltpu.make_async_remote_copy(
            src_ref=xsend.at[to], dst_ref=xrecv.at[me], send_sem=xs_sem, recv_sem=xr_sem,
            device_id={"seq": to}, device_id_type=MESH,
        ).start()
        return carry

    lax.fori_loop(1, n, send_x, 0)
    xrecv[pl.ds(me, 1)] = xsend[pl.ds(me, 1)]

    pad = jnp.zeros((LANES - wl_ref.shape[0] - 2, width), jnp.float32)
    stacked = jnp.concatenate([wl_ref[...], rate_ref[...], skip_ref[...], pad], 0)
    params[...] = stacked.T
    own = params[pl.ds(pl.multiple_of(me * group, group), group), :]
    hidden = wl_ref.shape[0]
    rate = own[:, hidden : hidden + 1]
    freq = freq_ref[...]
    wfb = jnp.concatenate(
        [wf_ref[...], bf_ref[...], jnp.zeros((40 - wf_ref.shape[0] - 1, hidden), jnp.float32)], 0
    ) * freq
    wm = wm_ref[...] * freq
    step = 512
    for j in range(K // step):
        cols = slice(j * step, (j + 1) * step)
        first = sine(dot_t(wfb, feat_ref[:, cols]))
        second = sine(dot_t(wm, first))
        raw = jnp.dot(
            own[:, :hidden], second, precision=lax.Precision.HIGHEST, preferred_element_type=jnp.float32
        )
        t = (lax.broadcasted_iota(jnp.int32, (group, step), 1) + j * step).astype(jnp.float32)
        taps_here = (raw * jnp.exp(-rate * t)).astype(jnp.bfloat16).astype(jnp.float32)
        h_ref[:, :, cols] = jnp.broadcast_to(taps_here[:, None], (group, 8, step))
    skip_col = jnp.broadcast_to(own[:, hidden + 1 : hidden + 2], (group, LANES))
    skips[...] = jnp.broadcast_to(skip_col[:, None], (group, 8, LANES))

    upper = lax.broadcasted_iota(jnp.int32, (LANES, LANES), 1) >= lax.broadcasted_iota(
        jnp.int32, (LANES, LANES), 0
    )
    taps = K // LANES

    def build(c, carry):
        last = jnp.zeros((LANES, LANES), jnp.float32)
        for m in range(taps + 1):
            if m < taps:
                line = rows_of(h_ref[c, :, m * LANES : (m + 1) * LANES], LANES)
                rolled = pltpu.roll(line, 0, 1, stride=1, stride_axis=0)
            else:
                rolled = jnp.zeros((LANES, LANES), jnp.float32)
            toep[c, m * LANES : (m + 1) * LANES, :] = jnp.where(upper, rolled, last).astype(jnp.bfloat16)
            last = rolled
        return carry

    lax.fori_loop(0, group, build, 0)

    every = pl.ds(0, n - 1)
    pltpu.make_async_remote_copy(
        src_ref=xsend.at[every], dst_ref=xrecv.at[every], send_sem=xs_sem, recv_sem=xr_sem,
        device_id={"seq": lax.rem(me + 1, n)}, device_id_type=MESH,
    ).wait()
    blocks = 2 * n
    front = taps * group
    xf[:front, :] = jnp.zeros((front, LANES), jnp.float32)
    xf[front:, :] = xrecv[...].astype(jnp.float32).reshape(blocks * group, LANES)

    def convolve(c, carry):
        pieces = [
            xf[pl.ds((taps - m) * group + c, blocks, stride=group), :] for m in range(taps + 1)
        ]
        lhs = jnp.concatenate([p.astype(jnp.bfloat16) for p in pieces], 1)
        y = jnp.dot(lhs, toep[c], preferred_element_type=jnp.float32)
        yf[pl.ds(c, blocks, stride=group), :] = y + rows_of(skips[c], blocks) * pieces[0]
        return carry

    lax.fori_loop(0, group, convolve, 0)
    ysend[...] = yf[...].reshape(n, 2 * group, LANES).astype(jnp.bfloat16)

    def send_y(k, carry):
        to = lax.rem(me + k, n)
        pltpu.make_async_remote_copy(
            src_ref=ysend.at[to], dst_ref=yrecv.at[me], send_sem=ys_sem, recv_sem=yr_sem,
            device_id={"seq": to}, device_id_type=MESH,
        ).start()
        return carry

    lax.fori_loop(1, n, send_y, 0)
    yrecv[pl.ds(me, 1)] = ysend[pl.ds(me, 1)]
    loads[1].wait()
    loads[2].wait()
    pltpu.make_async_remote_copy(
        src_ref=ysend.at[every], dst_ref=yrecv.at[every], send_sem=ys_sem, recv_sem=yr_sem,
        device_id={"seq": lax.rem(me + 1, n)}, device_id_type=MESH,
    ).wait()

    y = yrecv[...].astype(jnp.float32).reshape(n, 2, group, LANES)
    for r in range(2):
        here = slice(r * LANES, (r + 1) * LANES)
        v = y[:, r].reshape(n * group, LANES).T
        mixed[here, :] = (gate[here, :].astype(jnp.float32) * v).astype(jnp.bfloat16)

    copies = []
    for i, k in enumerate((2, 1, 3)):
        to = lax.rem(hd + k, heads)
        cols = pl.ds(pl.multiple_of(to * width, width), width)
        psend[i] = jnp.dot(mixed[...], w[:, cols], preferred_element_type=jnp.float32).astype(jnp.bfloat16)
        copy = pltpu.make_async_remote_copy(
            src_ref=psend.at[i], dst_ref=precv.at[i], send_sem=ps_sems.at[i], recv_sem=pr_sems.at[i],
            device_id={"head": to}, device_id_type=MESH,
        )
        copy.start()
        copies.append(copy)
    cols = pl.ds(pl.multiple_of(hd * width, width), width)
    part[...] = jnp.dot(mixed[...], w[:, cols], preferred_element_type=jnp.float32)
    for copy in copies:
        copy.wait()
    total = part[...]
    for i in range(heads - 1):
        total = total + precv[i].astype(jnp.float32)
    out_ref[...] = total.astype(jnp.bfloat16)


def local(signal, gate, skip, w_first, b_first, freq, w_mid, w_last, rate, out_w):
    n, heads = lax.axis_size("seq"), lax.axis_size("head")
    rows, width = signal.shape
    group = width // n
    bf16, f32 = jnp.bfloat16, jnp.float32
    vmem = pl.BlockSpec(memory_space=pltpu.VMEM)
    hbm = pl.BlockSpec(memory_space=pl.ANY)
    dma = pltpu.SemaphoreType.DMA
    return pl.pallas_call(
        functools.partial(kernel, n, heads),
        out_shape=jax.ShapeDtypeStruct((rows, width), bf16),
        in_specs=[hbm, hbm, vmem, vmem, vmem, vmem, vmem, vmem, vmem, hbm, vmem],
        out_specs=vmem,
        scratch_shapes=[
            pltpu.VMEM((rows, width), bf16),
            pltpu.VMEM((rows, width), bf16),
            pltpu.VMEM(out_w.shape, bf16),
            pltpu.VMEM((n, 2 * group, LANES), bf16),
            pltpu.VMEM((n, 2 * group, LANES), bf16),
            pltpu.VMEM(((2 * n + K // LANES) * group, LANES), f32),
            pltpu.VMEM((width, LANES), f32),
            pltpu.VMEM((group, 8, K), f32),
            pltpu.VMEM((group, 8, LANES), f32),
            pltpu.VMEM((group, K + LANES, LANES), bf16),
            pltpu.VMEM((2 * n * group, LANES), f32),
            pltpu.VMEM((n, 2 * group, LANES), bf16),
            pltpu.VMEM((n, 2 * group, LANES), bf16),
            pltpu.VMEM((rows, width), bf16),
            pltpu.VMEM((rows, width), f32),
            pltpu.VMEM((heads - 1, rows, width), bf16),
            pltpu.VMEM((heads - 1, rows, width), bf16),
            dma((3,)), dma, dma, dma, dma, dma((heads - 1,)), dma((heads - 1,)),
        ],
        compiler_params=pltpu.CompilerParams(collective_id=0, has_side_effects=True),
    )(
        signal, gate, skip[None], w_first, b_first[None], freq[None], w_mid, w_last, rate[None], out_w,
        jnp.asarray(features()),
    )


def solution(mesh):
    placed = (
        P("seq", "head"),
        P("seq", "head"),
        P("head"),
        P(),
        P(),
        P(),
        P(),
        P(None, "head"),
        P("head"),
        P("head", None),
    )
    return jax.shard_map(
        local, mesh=mesh, in_specs=placed, out_specs=P("seq", "head"), check_vma=False
    )
```

time: 163 us -> 52.1 us (0.32)
  the two profiles are of different devices: /device:TPU:2 before, /device:TPU:1 now
where the time goes in v1:
time: 52.1 us; the launch traced here: 51.9 us
  Pallas kernels  50.3 us (97%)
  local copies, waits for them, and re-layouts  1.67 us (3%)
    pallas_call x1, Pallas kernels, local(): pl.pallas_call(functools.partial(kernel, n, heads), out_shape=jax.ShapeDt...  50.3 us
    unnamed x1, local copies, waits for them, and re-layouts  1.67 us

profile of v1, /device:TPU:1, one launch (start us, length us, event | category | flops | bytes accessed | tf_op | source)
XLA Modules:
  0.0 51.9 jit_solution(1216696519811633718)
XLA Ops:
  0.0 50.3 %shard_map.109 = bf16[256,512]{1,0:T(8,128)(2,1)} custom-call(bf16[256,512]{1,0:T(8,128)(2,1)} %sig_hbm.1, bf16[256,512]{1,0:T(8,128)(2,1)} %gate_hbm.1, f32[1,512]{1,0:T(1,128)} %bitcast.4, f32[33,64]{1,0:T(8,128)} %wf_ref.1, f32[1,64]{1,0:T(1,128)} %bitcast.6, f32[1,64]{1,0:T(1,128)} %bitcast.7, f32[64,64]{1,0:T(8,128)} %wm_ref.1, f32[64,512]{1,0:T(8,128)} %wl_ref.1, ...), custom_call_target="tpu_custom_call" | custom-call | tf_op jit(solution)/shard_map/pallas_call | solution.py:216
  50.3 1.7 %copy.13 = bf16[256,512]{1,0:T(8,128)(2,1)} copy(bf16[256,512]{1,0:T(8,128)(2,1)} %shard_map.109) | data formatting | bytes 524288

commit v2 on v1

--- a/solution.py
+++ b/solution.py
@@ -12,6 +12,7 @@
 K = 2048
 BANDS = 16
 LANES = 128
+ZS = 8
 MESH = pl.DeviceIdType.MESH
 
 
@@ -51,19 +52,32 @@
 def kernel(
     n, heads, sig_hbm, gate_hbm, skip_ref, wf_ref, bf_ref, freq_ref, wm_ref, wl_ref, rate_ref, w_hbm, feat_ref,
     out_ref,
-    sig, gate, w, xsend, xrecv, xf, params, h_ref, skips, toep, yf, ysend, yrecv, mixed, part, psend, precv,
-    in_sems, xs_sem, xr_sem, ys_sem, yr_sem, ps_sems, pr_sems,
+    sig, gate, wc, xsend, xrecv, xf, params, h_ref, skips, toep, yf, ysend, yrecv, mixed, part,
+    in_sems, xs_sem, xr_sem, ys_sem, yr_sems, ws_sems, wr_sems, fs_sems, fr_sems, gs_sems, gr_sems,
 ):
     me = lax.axis_index("seq")
     hd = lax.axis_index("head")
     group = xsend.shape[1] // 2
-    rows = sig.shape[0]
-    width = sig.shape[1]
-
+    rows, width = sig.shape
+    pairs = width // LANES
+    per_pair = n // pairs
+
+    y, z, core = me // (2 * ZS), lax.rem(me // 2, ZS), lax.rem(me, 2)
+    ys = n // (2 * ZS)
+    pair = z // 2
+    own_group = z * (2 * ys) + y * 2 + core
+
+    def peer(q, k):
+        pz = lax.rem(pair + q, pairs) * 2 + lax.rem(z + k // (2 * ys), 2)
+        py = lax.rem(y + lax.rem(k // 2, ys), ys)
+        pc = lax.rem(core + k, 2)
+        return py * (2 * ZS) + pz * 2 + pc, pz * (2 * ys) + py * 2 + pc
+
+    cols = pl.ds(pl.multiple_of(hd * width, width), width)
     loads = [
         pltpu.make_async_copy(sig_hbm, sig, in_sems.at[0]),
         pltpu.make_async_copy(gate_hbm, gate, in_sems.at[1]),
-        pltpu.make_async_copy(w_hbm, w, in_sems.at[2]),
+        pltpu.make_async_copy(w_hbm.at[:, cols], wc.at[hd], in_sems.at[2]),
     ]
     for c in loads:
         c.start()
@@ -84,21 +98,35 @@
 
     pl.semaphore_wait(barrier, n - 1 + heads - 1)
 
-    def send_x(k, carry):
-        to = lax.rem(me + k, n)
-        pltpu.make_async_remote_copy(
-            src_ref=xsend.at[to], dst_ref=xrecv.at[me], send_sem=xs_sem, recv_sem=xr_sem,
-            device_id={"seq": to}, device_id_type=MESH,
-        ).start()
-        return carry
-
-    lax.fori_loop(1, n, send_x, 0)
-    xrecv[pl.ds(me, 1)] = xsend[pl.ds(me, 1)]
+    for q in (2, 1, 3, 0):
+
+        def send_x(k, carry, q=q):
+            to, slot = peer(q, k)
+            pltpu.make_async_remote_copy(
+                src_ref=xsend.at[slot], dst_ref=xrecv.at[me], send_sem=xs_sem, recv_sem=xr_sem,
+                device_id={"seq": to}, device_id_type=MESH,
+            ).start()
+            return carry
+
+        lax.fori_loop(0 if q else 1, per_pair, send_x, 0)
+    xrecv[pl.ds(me, 1)] = xsend[pl.ds(own_group, 1)]
+
+    half = pl.ds(pl.multiple_of(core * (width // 2), width // 2), width // 2)
+    fetches = []
+    for i, k in enumerate((2, 1, 3)):
+        to = lax.rem(hd + k, heads)
+        there = pl.ds(pl.multiple_of(to * width, width), width)
+        fetch = pltpu.make_async_remote_copy(
+            src_ref=w_hbm.at[half, there], dst_ref=wc.at[hd, half], send_sem=ws_sems.at[i],
+            recv_sem=wr_sems.at[i], device_id={"head": to}, device_id_type=MESH,
+        )
+        fetch.start()
+        fetches.append(fetch)
 
     pad = jnp.zeros((LANES - wl_ref.shape[0] - 2, width), jnp.float32)
     stacked = jnp.concatenate([wl_ref[...], rate_ref[...], skip_ref[...], pad], 0)
     params[...] = stacked.T
-    own = params[pl.ds(pl.multiple_of(me * group, group), group), :]
+    own = params[pl.ds(pl.multiple_of(own_group * group, group), group), :]
     hidden = wl_ref.shape[0]
     rate = own[:, hidden : hidden + 1]
     freq = freq_ref[...]
@@ -108,15 +136,15 @@
     wm = wm_ref[...] * freq
     step = 512
     for j in range(K // step):
-        cols = slice(j * step, (j + 1) * step)
-        first = sine(dot_t(wfb, feat_ref[:, cols]))
+        here = slice(j * step, (j + 1) * step)
+        first = sine(dot_t(wfb, feat_ref[:, here]))
         second = sine(dot_t(wm, first))
         raw = jnp.dot(
             own[:, :hidden], second, precision=lax.Precision.HIGHEST, preferred_element_type=jnp.float32
         )
         t = (lax.broadcasted_iota(jnp.int32, (group, step), 1) + j * step).astype(jnp.float32)
         taps_here = (raw * jnp.exp(-rate * t)).astype(jnp.bfloat16).astype(jnp.float32)
-        h_ref[:, :, cols] = jnp.broadcast_to(taps_here[:, None], (group, 8, step))
+        h_ref[:, :, here] = jnp.broadcast_to(taps_here[:, None], (group, 8, step))
     skip_col = jnp.broadcast_to(own[:, hidden + 1 : hidden + 2], (group, LANES))
     skips[...] = jnp.broadcast_to(skip_col[:, None], (group, 8, LANES))
 
@@ -154,55 +182,102 @@
             xf[pl.ds((taps - m) * group + c, blocks, stride=group), :] for m in range(taps + 1)
         ]
         lhs = jnp.concatenate([p.astype(jnp.bfloat16) for p in pieces], 1)
-        y = jnp.dot(lhs, toep[c], preferred_element_type=jnp.float32)
-        yf[pl.ds(c, blocks, stride=group), :] = y + rows_of(skips[c], blocks) * pieces[0]
+        conv = jnp.dot(lhs, toep[c], preferred_element_type=jnp.float32)
+        yf[pl.ds(c, blocks, stride=group), :] = conv + rows_of(skips[c], blocks) * pieces[0]
         return carry
 
     lax.fori_loop(0, group, convolve, 0)
     ysend[...] = yf[...].reshape(n, 2 * group, LANES).astype(jnp.bfloat16)
 
-    def send_y(k, carry):
-        to = lax.rem(me + k, n)
-        pltpu.make_async_remote_copy(
-            src_ref=ysend.at[to], dst_ref=yrecv.at[me], send_sem=ys_sem, recv_sem=yr_sem,
-            device_id={"seq": to}, device_id_type=MESH,
-        ).start()
-        return carry
-
-    lax.fori_loop(1, n, send_y, 0)
-    yrecv[pl.ds(me, 1)] = ysend[pl.ds(me, 1)]
+    order = (0, 1, 3, 2)
+    for q in order:
+
+        def send_y(k, carry, q=q):
+            to, slot = peer(q, k)
+            pltpu.make_async_remote_copy(
+                src_ref=ysend.at[to], dst_ref=yrecv.at[own_group], send_sem=ys_sem, recv_sem=yr_sems.at[pair],
+                device_id={"seq": to}, device_id_type=MESH,
+            ).start()
+            return carry
+
+        lax.fori_loop(0 if q else 1, per_pair, send_y, 0)
+    yrecv[pl.ds(own_group, 1)] = ysend[pl.ds(me, 1)]
+
+    partner = me + 1 - 2 * core
+    passes = []
+    for i, k in enumerate((2, 1, 3)):
+        fetches[i].wait()
+        whose = lax.rem(hd + heads - k, heads)
+        onward = pltpu.make_async_remote_copy(
+            src_ref=wc.at[whose, half], dst_ref=wc.at[whose, half], send_sem=fs_sems.at[i],
+            recv_sem=fr_sems.at[i], device_id={"seq": partner}, device_id_type=MESH,
+        )
+        onward.start()
+        passes.append(onward)
     loads[1].wait()
     loads[2].wait()
-    pltpu.make_async_remote_copy(
-        src_ref=ysend.at[every], dst_ref=yrecv.at[every], send_sem=ys_sem, recv_sem=yr_sem,
-        device_id={"seq": lax.rem(me + 1, n)}, device_id_type=MESH,
-    ).wait()
-
-    y = yrecv[...].astype(jnp.float32).reshape(n, 2, group, LANES)
-    for r in range(2):
-        here = slice(r * LANES, (r + 1) * LANES)
-        v = y[:, r].reshape(n * group, LANES).T
-        mixed[here, :] = (gate[here, :].astype(jnp.float32) * v).astype(jnp.bfloat16)
-
-    copies = []
-    for i, k in enumerate((2, 1, 3)):
-        to = lax.rem(hd + k, heads)
-        cols = pl.ds(pl.multiple_of(to * width, width), width)
-        psend[i] = jnp.dot(mixed[...], w[:, cols], preferred_element_type=jnp.float32).astype(jnp.bfloat16)
-        copy = pltpu.make_async_remote_copy(
-            src_ref=psend.at[i], dst_ref=precv.at[i], send_sem=ps_sems.at[i], recv_sem=pr_sems.at[i],
+
+    right, left = lax.rem(hd + 1, heads), lax.rem(hd + heads - 1, heads)
+    top, low = pl.ds(0, rows // 2), pl.ds(rows // 2, rows // 2)
+
+    def hop(kind, b, ref, to):
+        return pltpu.make_async_remote_copy(
+            src_ref=ref, dst_ref=ref, send_sem=gs_sems.at[kind, b], recv_sem=gr_sems.at[kind, b],
             device_id={"head": to}, device_id_type=MESH,
         )
-        copy.start()
-        copies.append(copy)
-    cols = pl.ds(pl.multiple_of(hd * width, width), width)
-    part[...] = jnp.dot(mixed[...], w[:, cols], preferred_element_type=jnp.float32)
-    for copy in copies:
+
+    started = []
+
+    def onwards(b):
+        p = lax.rem(pair + order[b], pairs)
+        firsts[b][0].wait_recv()
+        started.append(hop(2, b, mixed.at[left, p, top], right))
+        started[-1].start()
+        firsts[b][1].wait_recv()
+        started.append(hop(3, b, mixed.at[right, p, low], left))
+        started[-1].start()
+
+    firsts = []
+    for b, q in enumerate(order):
+        p = lax.rem(pair + q, pairs)
+        count = per_pair if q else per_pair - 1
+        some = pl.ds(0, count)
+        pltpu.make_async_remote_copy(
+            src_ref=ysend.at[some], dst_ref=yrecv.at[some], send_sem=ys_sem, recv_sem=yr_sems.at[p],
+            device_id={"seq": partner}, device_id_type=MESH,
+        ).wait_recv()
+        v = yrecv[pl.ds(pl.multiple_of(p * per_pair, per_pair), per_pair)].astype(jnp.float32)
+        v = v.reshape(per_pair, 2, group, LANES)
+        channels = pl.ds(pl.multiple_of(p * LANES, LANES), LANES)
+        for r in range(2):
+            here = slice(r * LANES, (r + 1) * LANES)
+            vt = v[:, r].reshape(LANES, LANES).T
+            mixed[hd, p, here, :] = (gate[here, channels].astype(jnp.float32) * vt).astype(jnp.bfloat16)
+        firsts.append([hop(0, b, mixed.at[hd, p], right), hop(1, b, mixed.at[hd, p], left)])
+        for copy in firsts[b]:
+            copy.start()
+        if b:
+            onwards(b - 1)
+
+    def product(h):
+        lhs = jnp.concatenate([mixed[h, p] for p in range(pairs)], 1)
+        return jnp.dot(lhs, wc[h], preferred_element_type=jnp.float32)
+
+    for onward in passes:
+        onward.wait()
+    part[...] = product(hd)
+    onwards(pairs - 1)
+    part[...] += product(left) + product(right)
+    for copy in started:
         copy.wait()
-    total = part[...]
-    for i in range(heads - 1):
-        total = total + precv[i].astype(jnp.float32)
-    out_ref[...] = total.astype(jnp.bfloat16)
+    out_ref[...] = (part[...] + product(lax.rem(hd + 2, heads))).astype(jnp.bfloat16)
+    for copies in firsts:
+        for copy in copies:
+            copy.wait_send()
+    pltpu.make_async_remote_copy(
+        src_ref=ysend.at[every], dst_ref=yrecv.at[every], send_sem=ys_sem, recv_sem=yr_sems.at[0],
+        device_id={"seq": partner}, device_id_type=MESH,
+    ).wait_send()
 
 
 def local(signal, gate, skip, w_first, b_first, freq, w_mid, w_last, rate, out_w):
@@ -221,7 +296,7 @@
         scratch_shapes=[
             pltpu.VMEM((rows, width), bf16),
             pltpu.VMEM((rows, width), bf16),
-            pltpu.VMEM(out_w.shape, bf16),
+            pltpu.VMEM((heads, width, width), bf16),
             pltpu.VMEM((n, 2 * group, LANES), bf16),
             pltpu.VMEM((n, 2 * group, LANES), bf16),
             pltpu.VMEM(((2 * n + K // LANES) * group, LANES), f32),
@@ -232,11 +307,10 @@
             pltpu.VMEM((2 * n * group, LANES), f32),
             pltpu.VMEM((n, 2 * group, LANES), bf16),
             pltpu.VMEM((n, 2 * group, LANES), bf16),
-            pltpu.VMEM((rows, width), bf16),
+            pltpu.VMEM((heads, width // LANES, rows, LANES), bf16),
             pltpu.VMEM((rows, width), f32),
-            pltpu.VMEM((heads - 1, rows, width), bf16),
-            pltpu.VMEM((heads - 1, rows, width), bf16),
-            dma((3,)), dma, dma, dma, dma, dma((heads - 1,)), dma((heads - 1,)),
+            dma((3,)), dma, dma, dma, dma((width // LANES,)), dma((heads - 1,)), dma((heads - 1,)),
+            dma((heads - 1,)), dma((heads - 1,)), dma((4, width // LANES)), dma((4, width // LANES)),
         ],
         compiler_params=pltpu.CompilerParams(collective_id=0, has_side_effects=True),
     )(

time: 52.1 us -> 46.6 us (0.89)
  the two profiles are of different devices: /device:TPU:1 before, /device:TPU:2 now
where the time goes in v2:
time: 46.6 us; the launch traced here: 46.1 us
  Pallas kernels  44.4 us (95%)
  local copies, waits for them, and re-layouts  1.67 us (4%)
    pallas_call x1, Pallas kernels, local(): pl.pallas_call(functools.partial(kernel, n, heads), out_shape=jax.ShapeDt...  44.4 us
    unnamed x1, local copies, waits for them, and re-layouts  1.67 us

profile of v2, /device:TPU:2, one launch (start us, length us, event | category | flops | bytes accessed | tf_op | source)
XLA Modules:
  0.0 46.1 jit_solution(13315339981472307691)
XLA Ops:
  0.0 44.4 %shard_map.109 = bf16[256,512]{1,0:T(8,128)(2,1)} custom-call(bf16[256,512]{1,0:T(8,128)(2,1)} %sig_hbm.1, bf16[256,512]{1,0:T(8,128)(2,1)} %gate_hbm.1, f32[1,512]{1,0:T(1,128)} %bitcast.4, f32[33,64]{1,0:T(8,128)} %wf_ref.1, f32[1,64]{1,0:T(1,128)} %bitcast.6, f32[1,64]{1,0:T(1,128)} %bitcast.7, f32[64,64]{1,0:T(8,128)} %wm_ref.1, f32[64,512]{1,0:T(8,128)} %wl_ref.1, ...), custom_call_target="tpu_custom_call" | custom-call | tf_op jit(solution)/shard_map/pallas_call | solution.py:291
  44.4 1.7 %copy.13 = bf16[256,512]{1,0:T(8,128)(2,1)} copy(bf16[256,512]{1,0:T(8,128)(2,1)} %shard_map.109) | data formatting | bytes 524288

commit v3 on v2

v3 whole, which is shorter than its diff:
```python
import functools
import math

import jax
import jax.numpy as jnp
import numpy as np
from jax import lax
from jax.experimental import pallas as pl
from jax.experimental.pallas import tpu as pltpu
from jax.sharding import PartitionSpec as P

K = 2048
BANDS = 16
LANES = 128
ZS = 8
MESH = pl.DeviceIdType.MESH


def features():
    t = np.arange(K, dtype=np.float64)
    bands = np.arange(1, BANDS + 1, dtype=np.float64)
    angles = 2.0 * math.pi * t[None, :] * bands[:, None] / K
    rows = np.concatenate([t[None] / K, np.cos(angles), np.sin(angles), np.ones((1, K))], 0)
    rows = np.concatenate([rows, np.zeros((40 - rows.shape[0], K))], 0)
    return rows.astype(np.float32)


def sine(x):
    turns = jnp.round(x * (1.0 / math.pi))
    r = (x - turns * 3.140625) - turns * (math.pi - 3.140625)
    s = r * r
    p = -1.0 / 39916800.0
    for c in (1.0 / 362880.0, -1.0 / 5040.0, 1.0 / 120.0, -1.0 / 6.0):
        p = p * s + c
    v = r + r * s * p
    odd = jnp.bitwise_and(turns.astype(jnp.int32), 1)
    return jnp.where(odd == 1, -v, v)


def rows_of(tile, count):
    copies = jnp.broadcast_to(tile[None], (count // tile.shape[0], *tile.shape))
    return copies.reshape(count, tile.shape[1])


def dot_t(a, b):
    return lax.dot_general(
        a, b, (((0,), (0,)), ((), ())),
        precision=lax.Precision.HIGHEST, preferred_element_type=jnp.float32,
    )


def swap_halves(one, two):
    upper = lax.broadcasted_iota(jnp.int32, one.shape, 1) < 4
    moved_one, moved_two = pltpu.roll(one, 4, 1), pltpu.roll(two, 4, 1)
    return jnp.where(upper, one, moved_two), jnp.where(upper, moved_one, two)


def kernel(
    n, heads, sig_hbm, gate_hbm, skip_hbm, wf_hbm, bf_hbm, freq_hbm, wm_hbm, wl_hbm, rate_hbm, w_hbm, feat_hbm,
    out_ref,
    sig, gate, skip_ref, wf_ref, bf_ref, freq_ref, wm_ref, wl_ref, rate_ref, feat_ref,
    wc, wrelay, xsend, xrecv, xf, params, h_ref, skips, toep, yf, ysend, yrecv, mixed, part,
    in_sems, xs_sems, xr_sems, ys_sems, yr_sems, ws_sems, wr_sems, fs_sems, fr_sems, gs_sems, gr_sems,
):
    me = lax.axis_index("seq")
    hd = lax.axis_index("head")
    rows, width = sig.shape
    group = width // n
    part_group = group // 2
    chunks = width // LANES
    per_chunk = n // 2
    taps = K // LANES
    blocks = 2 * n

    ys = n // (2 * ZS)
    y, z, core = me // (2 * ZS), lax.rem(me // 2, ZS), lax.rem(me, 2)
    z_half, z_low = z // 4, lax.rem(z, 4)
    own_group = z * (2 * ys) + y * 2 + core
    y_at = [lax.rem(y + i, ys) for i in range(ys)]
    core_at = [core, 1 - core]

    def peers(z_list, own_first):
        found = []
        for i, pz in enumerate(z_list):
            for dy in (2, 1, 3, 0):
                for dc in (1, 0):
                    if not (own_first and i == len(z_list) - 1 and dy == 0 and dc == 0):
                        found.append((
                            y_at[dy] * (2 * ZS) + pz * 2 + core_at[dc],
                            pz * (2 * ys) + y_at[dy] * 2 + core_at[dc],
                        ))
        return found

    everyone = peers([lax.rem(z + i, ZS) for i in (4, 3, 5, 2, 6, 1, 7, 0)], True)
    near = peers([z_half * 4 + lax.rem(z_low + i, 4) for i in (2, 1, 3, 0)], True)
    far = peers([(1 - z_half) * 4 + lax.rem(z_low + i, 4) for i in (0, 1, 3, 2)], False)

    barrier = pltpu.get_barrier_semaphore()
    load_sig = pltpu.make_async_copy(sig_hbm, sig, in_sems.at[0])
    load_sig.start()
    for to, _ in everyone:
        pl.semaphore_signal(barrier, inc=1, device_id={"seq": to}, device_id_type=MESH)
    right, left, opp = lax.rem(hd + 1, heads), lax.rem(hd + heads - 1, heads), lax.rem(hd + 2, heads)
    for to in (opp, right, left):
        pl.semaphore_signal(barrier, inc=1, device_id={"head": to}, device_id_type=MESH)

    def columns(h):
        return pl.ds(pl.multiple_of(h * width, width), width)

    small = (
        (wf_hbm, wf_ref), (bf_hbm, bf_ref), (freq_hbm, freq_ref), (wm_hbm, wm_ref), (wl_hbm, wl_ref),
        (rate_hbm, rate_ref), (skip_hbm, skip_ref), (feat_hbm, feat_ref),
        (gate_hbm, gate), (w_hbm.at[:, columns(hd)], wc.at[hd]),
    )
    loads = [pltpu.make_async_copy(src, dst, in_sems.at[i + 1]) for i, (src, dst) in enumerate(small)]
    for load in loads:
        load.start()

    load_sig.wait()
    xt = sig[...].astype(jnp.float32).T
    for h in range(2):
        piece = xt[h * (width // 2) : (h + 1) * (width // 2)].reshape(n // 2, 8, rows)
        one, two = swap_halves(piece[:, :, :LANES], piece[:, :, LANES:])
        xsend[h] = jnp.stack([one, two], 1).reshape(n, 8, LANES).astype(jnp.bfloat16)

    pl.semaphore_wait(barrier, n - 1 + heads - 1)

    for h in range(2):
        for to, slot in everyone:
            pltpu.make_async_remote_copy(
                src_ref=xsend.at[h, slot], dst_ref=xrecv.at[h, me], send_sem=xs_sems.at[h],
                recv_sem=xr_sems.at[h], device_id={"seq": to}, device_id_type=MESH,
            ).start()
    for h in range(2):
        xrecv[h, pl.ds(me, 1)] = xsend[h, pl.ds(own_group, 1)]

    half = pl.ds(pl.multiple_of(core * (width // 2), width // 2), width // 2)
    quarters = [
        pl.ds(pl.multiple_of(core * (width // 2) + i * (width // 4), width // 4), width // 4) for i in range(2)
    ]

    def fetch(i, src, dst, to):
        return pltpu.make_async_remote_copy(
            src_ref=src, dst_ref=dst, send_sem=ws_sems.at[i], recv_sem=wr_sems.at[i],
            device_id={"head": to}, device_id_type=MESH,
        )

    fetches = [
        fetch(0, w_hbm.at[quarters[0], columns(opp)], wrelay.at[0], right),
        fetch(1, w_hbm.at[quarters[1], columns(opp)], wrelay.at[1], left),
        fetch(2, w_hbm.at[half, columns(right)], wc.at[hd, half], right),
        fetch(3, w_hbm.at[half, columns(left)], wc.at[hd, half], left),
        fetch(4, wrelay.at[0], wc.at[left, quarters[0]], right),
        fetch(5, wrelay.at[1], wc.at[right, quarters[1]], left),
    ]
    for i in range(4):
        fetches[i].start()

    for load in loads[:8]:
        load.wait()
    pad = jnp.zeros((LANES - wl_ref.shape[0] - 2, width), jnp.float32)
    stacked = jnp.concatenate([wl_ref[...], rate_ref[...], skip_ref[...], pad], 0)
    params[...] = stacked.T
    pair = own_group - core
    lower, upper = [
        params[pl.ds(pl.multiple_of(pair * part_group + h * (width // 2), 8), 8), :] for h in range(2)
    ]
    first_rows = lax.broadcasted_iota(jnp.int32, (8, LANES), 0) < 4
    even = jnp.where(first_rows, lower, pltpu.roll(upper, 4, 0))
    odd = jnp.where(first_rows, pltpu.roll(lower, 4, 0), upper)
    own = jnp.where(core == 0, even, odd)
    hidden = wl_ref.shape[0]
    rate = own[:, hidden : hidden + 1]
    freq = freq_ref[...]
    wfb = jnp.concatenate(
        [wf_ref[...], bf_ref[...], jnp.zeros((40 - wf_ref.shape[0] - 1, hidden), jnp.float32)], 0
    ) * freq
    wm = wm_ref[...] * freq
    step = 512
    for j in range(K // step):
        here = slice(j * step, (j + 1) * step)
        first = sine(dot_t(wfb, feat_ref[:, here]))
        second = sine(dot_t(wm, first))
        raw = jnp.dot(
            own[:, :hidden], second, precision=lax.Precision.HIGHEST, preferred_element_type=jnp.float32
        )
        t = (lax.broadcasted_iota(jnp.int32, (group, step), 1) + j * step).astype(jnp.float32)
        taps_here = (raw * jnp.exp(-rate * t)).astype(jnp.bfloat16).astype(jnp.float32)
        h_ref[:, :, here] = jnp.broadcast_to(taps_here[:, None], (group, 8, step))
    skip_col = jnp.broadcast_to(own[:, hidden + 1 : hidden + 2], (group, LANES))
    skips[...] = jnp.broadcast_to(skip_col[:, None], (group, 8, LANES))

    causal = lax.broadcasted_iota(jnp.int32, (LANES, LANES), 1) >= lax.broadcasted_iota(
        jnp.int32, (LANES, LANES), 0
    )

    def build(c, carry):
        last = jnp.zeros((LANES, LANES), jnp.float32)
        for m in range(taps + 1):
            if m < taps:
                line = rows_of(h_ref[c, :, m * LANES : (m + 1) * LANES], LANES)
                rolled = pltpu.roll(line, 0, 1, stride=1, stride_axis=0)
            else:
                rolled = jnp.zeros((LANES, LANES), jnp.float32)
            toep[c, m * LANES : (m + 1) * LANES, :] = jnp.where(causal, rolled, last).astype(jnp.bfloat16)
            last = rolled
        return carry

    lax.fori_loop(0, group, build, 0)

    every = pl.ds(0, n - 1)
    front = taps * part_group
    partner = me + 1 - 2 * core

    def exchanged(h):
        return pltpu.make_async_remote_copy(
            src_ref=xsend.at[h, every], dst_ref=xrecv.at[h, every], send_sem=xs_sems.at[h],
            recv_sem=xr_sems.at[h], device_id={"seq": partner}, device_id_type=MESH,
        )

    for h in range(2):
        exchanged(h).wait_recv()
        xf[h, :front, :] = jnp.zeros((front, LANES), jnp.float32)
        xf[h, front:, :] = xrecv[h].astype(jnp.float32).reshape(blocks * part_group, LANES)

        def convolve(c, carry, h=h):
            pieces = [
                xf[h, pl.ds((taps - m) * part_group + c, blocks, stride=part_group), :] for m in range(taps + 1)
            ]
            lhs = jnp.concatenate([p.astype(jnp.bfloat16) for p in pieces], 1)
            channel = c + h * part_group
            conv = jnp.dot(lhs, toep[channel], preferred_element_type=jnp.float32)
            yf[h, pl.ds(c, blocks, stride=part_group), :] = conv + rows_of(skips[channel], blocks) * pieces[0]
            return carry

        lax.fori_loop(0, part_group, convolve, 0)
        ysend[h] = yf[h].reshape(n, 8, LANES).astype(jnp.bfloat16)
        for to, _ in near + far:
            pltpu.make_async_remote_copy(
                src_ref=ysend.at[h, to], dst_ref=yrecv.at[h, own_group], send_sem=ys_sems.at[h],
                recv_sem=yr_sems.at[h, z_half], device_id={"seq": to}, device_id_type=MESH,
            ).start()
        yrecv[h, pl.ds(own_group, 1)] = ysend[h, pl.ds(me, 1)]

    for i in range(2):
        fetches[i].wait_recv()
        fetches[4 + i].start()

    def onward(i, ref):
        return pltpu.make_async_remote_copy(
            src_ref=ref, dst_ref=ref, send_sem=fs_sems.at[i], recv_sem=fr_sems.at[i],
            device_id={"seq": partner}, device_id_type=MESH,
        )

    passes = [onward(0, wc.at[left, half]), onward(1, wc.at[right, half]), onward(2, wc.at[opp, half])]
    loads[8].wait()

    top, low = pl.ds(0, rows // 2), pl.ds(rows // 2, rows // 2)

    def hop(kind, b, ref, to):
        return pltpu.make_async_remote_copy(
            src_ref=ref, dst_ref=ref, send_sem=gs_sems.at[kind, b], recv_sem=gr_sems.at[kind, b],
            device_id={"head": to}, device_id_type=MESH,
        )

    order = [(h, z_half if g == 0 else 1 - z_half, g) for h in range(2) for g in range(2)]
    firsts, seconds = [], []

    def onwards(b):
        p = order[b][0] * 2 + order[b][1]
        firsts[b][0].wait_recv()
        seconds.append(hop(2, b, mixed.at[left, p, top], right))
        seconds[-1].start()
        firsts[b][1].wait_recv()
        seconds.append(hop(3, b, mixed.at[right, p, low], left))
        seconds[-1].start()

    for b, (h, zs, g) in enumerate(order):
        p = h * 2 + zs
        some = pl.ds(0, per_chunk if g else per_chunk - 1)
        pltpu.make_async_remote_copy(
            src_ref=ysend.at[h, some], dst_ref=yrecv.at[h, some], send_sem=ys_sems.at[h],
            recv_sem=yr_sems.at[h, zs], device_id={"seq": partner}, device_id_type=MESH,
        ).wait_recv()
        v = yrecv[h, pl.ds(pl.multiple_of(zs * per_chunk, per_chunk), per_chunk)].astype(jnp.float32)
        v = v.reshape(per_chunk // 2, 2, 8, LANES)
        channels = pl.ds(pl.multiple_of(p * LANES, LANES), LANES)
        for r, piece in enumerate(swap_halves(v[:, 0], v[:, 1])):
            here = slice(r * LANES, (r + 1) * LANES)
            vt = piece.reshape(LANES, LANES).T
            mixed[hd, p, here, :] = (gate[here, channels].astype(jnp.float32) * vt).astype(jnp.bfloat16)
        firsts.append([hop(0, b, mixed.at[hd, p], right), hop(1, b, mixed.at[hd, p], left)])
        for copy in firsts[b]:
            copy.start()
        if b == 1:
            for i in range(2):
                fetches[2 + i].wait_recv()
                passes[i].start()
            onwards(0)

    def product(h):
        lhs = jnp.concatenate([mixed[h, p] for p in range(chunks)], 1)
        return jnp.dot(lhs, wc[h], preferred_element_type=jnp.float32)

    for i in range(2):
        fetches[4 + i].wait_recv()
    passes[2].start()
    loads[9].wait()
    onwards(1)
    part[...] = product(hd)
    onwards(2)
    onwards(3)
    for weights in passes:
        weights.wait_recv()
    part[...] += product(left) + product(right)
    for copy in seconds:
        copy.wait_recv()
    out_ref[...] = (part[...] + product(opp)).astype(jnp.bfloat16)

    for copies in (*firsts, seconds, passes, fetches):
        for copy in copies:
            copy.wait_send()
    for h in range(2):
        exchanged(h).wait_send()
        pltpu.make_async_remote_copy(
            src_ref=ysend.at[h, every], dst_ref=yrecv.at[h, every], send_sem=ys_sems.at[h],
            recv_sem=yr_sems.at[h, 0], device_id={"seq": partner}, device_id_type=MESH,
        ).wait_send()


def local(signal, gate, skip, w_first, b_first, freq, w_mid, w_last, rate, out_w):
    n, heads = lax.axis_size("seq"), lax.axis_size("head")
    rows, width = signal.shape
    group = width // n
    bf16, f32 = jnp.bfloat16, jnp.float32
    vmem = pl.BlockSpec(memory_space=pltpu.VMEM)
    hbm = pl.BlockSpec(memory_space=pl.ANY)
    dma = pltpu.SemaphoreType.DMA
    operands = (
        signal, gate, skip[None], w_first, b_first[None], freq[None], w_mid, w_last, rate[None], out_w,
        jnp.asarray(features()),
    )
    return pl.pallas_call(
        functools.partial(kernel, n, heads),
        out_shape=jax.ShapeDtypeStruct((rows, width), bf16),
        in_specs=[hbm] * 11,
        out_specs=vmem,
        scratch_shapes=[
            pltpu.VMEM((rows, width), bf16),
            pltpu.VMEM((rows, width), bf16),
            *[pltpu.VMEM(a.shape, a.dtype) for a in operands[2:9]],
            pltpu.VMEM(operands[10].shape, f32),
            pltpu.VMEM((heads, width, width), bf16),
            pltpu.VMEM((2, width // 4, width), bf16),
            pltpu.VMEM((2, n, group, LANES), bf16),
            pltpu.VMEM((2, n, group, LANES), bf16),
            pltpu.VMEM((2, (2 * n + K // LANES) * group // 2, LANES), f32),
            pltpu.VMEM((width, LANES), f32),
            pltpu.VMEM((group, 8, K), f32),
            pltpu.VMEM((group, 8, LANES), f32),
            pltpu.VMEM((group, K + LANES, LANES), bf16),
            pltpu.VMEM((2, n * group, LANES), f32),
            pltpu.VMEM((2, n, group, LANES), bf16),
            pltpu.VMEM((2, n, group, LANES), bf16),
            pltpu.VMEM((heads, width // LANES, rows, LANES), bf16),
            pltpu.VMEM((rows, width), f32),
            dma((11,)), dma((2,)), dma((2,)), dma((2,)), dma((2, 2)), dma((6,)), dma((6,)),
            dma((3,)), dma((3,)), dma((4, width // LANES)), dma((4, width // LANES)),
        ],
        compiler_params=pltpu.CompilerParams(collective_id=0, has_side_effects=True),
    )(*operands)


def solution(mesh):
    placed = (
        P("seq", "head"),
        P("seq", "head"),
        P("head"),
        P(),
        P(),
        P(),
        P(),
        P(None, "head"),
        P("head"),
        P("head", None),
    )
    return jax.shard_map(
        local, mesh=mesh, in_specs=placed, out_specs=P("seq", "head"), check_vma=False
    )
```

time: 46.6 us -> 41.8 us (0.90)
  Pallas kernels: 44.4 us -> 40 us
    pallas_call x1, Pallas kernels: 44.4 us -> 40 us  [local(): pl.pallas_call(functools.partial(kernel, n, heads), out_shape=jax.ShapeDt...]
where the time goes in v3:
time: 41.8 us; the launch traced here: 41.7 us
  Pallas kernels  40 us (96%)
  local copies, waits for them, and re-layouts  1.67 us (4%)
    pallas_call x1, Pallas kernels, local(): pl.pallas_call(functools.partial(kernel, n, heads), out_shape=jax.ShapeDt...  40 us
    unnamed x1, local copies, waits for them, and re-layouts  1.67 us

profile of v3, /device:TPU:2, one launch (start us, length us, event | category | flops | bytes accessed | tf_op | source)
XLA Modules:
  0.0 41.7 jit_solution(4409973538538280375)
XLA Ops:
  0.0 40.0 %shard_map.109 = bf16[256,512]{1,0:T(8,128)(2,1)} custom-call(bf16[256,512]{1,0:T(8,128)(2,1)} %sig_hbm.1, bf16[256,512]{1,0:T(8,128)(2,1)} %gate_hbm.1, f32[1,512]{1,0:T(1,128)} %bitcast.4, f32[33,64]{1,0:T(8,128)} %wf_hbm.1, f32[1,64]{1,0:T(1,128)} %bitcast.6, f32[1,64]{1,0:T(1,128)} %bitcast.7, f32[64,64]{1,0:T(8,128)} %wm_hbm.1, f32[64,512]{1,0:T(8,128)} %wl_hbm.1, ...), custom_call_target="tpu_custom_call" | custom-call | tf_op jit(solution)/shard_map/pallas_call | solution.py:343
  40.0 1.7 %copy.13 = bf16[256,512]{1,0:T(8,128)(2,1)} copy(bf16[256,512]{1,0:T(8,128)(2,1)} %shard_map.109) | data formatting | bytes 524288

commit v4 on v3

--- a/solution.py
+++ b/solution.py
@@ -264,10 +264,11 @@
         )
 
     order = [(h, z_half if g == 0 else 1 - z_half, g) for h in range(2) for g in range(2)]
+    chunk_of = [h * 2 + zs for h, zs, _ in order]
     firsts, seconds = [], []
 
     def onwards(b):
-        p = order[b][0] * 2 + order[b][1]
+        p = chunk_of[b]
         firsts[b][0].wait_recv()
         seconds.append(hop(2, b, mixed.at[left, p, top], right))
         seconds[-1].start()
@@ -276,7 +277,7 @@
         seconds[-1].start()
 
     for b, (h, zs, g) in enumerate(order):
-        p = h * 2 + zs
+        p = chunk_of[b]
         some = pl.ds(0, per_chunk if g else per_chunk - 1)
         pltpu.make_async_remote_copy(
             src_ref=ysend.at[h, some], dst_ref=yrecv.at[h, some], send_sem=ys_sems.at[h],
@@ -290,6 +291,8 @@
             vt = piece.reshape(LANES, LANES).T
             mixed[hd, p, here, :] = (gate[here, channels].astype(jnp.float32) * vt).astype(jnp.bfloat16)
         firsts.append([hop(0, b, mixed.at[hd, p], right), hop(1, b, mixed.at[hd, p], left)])
+        if b == chunks - 1:
+            firsts[b].append(hop(2, b, mixed.at[hd, p], opp))
         for copy in firsts[b]:
             copy.start()
         if b == 1:
@@ -298,24 +301,31 @@
                 passes[i].start()
             onwards(0)
 
-    def product(h):
-        lhs = jnp.concatenate([mixed[h, p] for p in range(chunks)], 1)
-        return jnp.dot(lhs, wc[h], preferred_element_type=jnp.float32)
+    def product_of_half(h, first):
+        lhs = jnp.concatenate([mixed[h, first], mixed[h, first + 1]], 1)
+        return jnp.dot(
+            lhs, wc[h, first * LANES : (first + 2) * LANES], preferred_element_type=jnp.float32
+        )
 
     for i in range(2):
         fetches[4 + i].wait_recv()
     passes[2].start()
     loads[9].wait()
     onwards(1)
-    part[...] = product(hd)
+    part[...] = product_of_half(hd, 0) + product_of_half(hd, 2)
     onwards(2)
-    onwards(3)
     for weights in passes:
         weights.wait_recv()
-    part[...] += product(left) + product(right)
-    for copy in seconds:
+    for b in range(2):
+        for copy in seconds[2 * b : 2 * b + 2]:
+            copy.wait_recv()
+    part[...] += product_of_half(left, 0) + product_of_half(right, 0) + product_of_half(opp, 0)
+    for copy in firsts[3][:2]:
         copy.wait_recv()
-    out_ref[...] = (part[...] + product(opp)).astype(jnp.bfloat16)
+    part[...] += product_of_half(left, 2) + product_of_half(right, 2)
+    for copy in (*seconds[4:], firsts[3][2]):
+        copy.wait_recv()
+    out_ref[...] = (part[...] + product_of_half(opp, 2)).astype(jnp.bfloat16)
 
     for copies in (*firsts, seconds, passes, fetches):
         for copy in copies:
@@ -342,7 +352,7 @@
     )
     return pl.pallas_call(
         functools.partial(kernel, n, heads),
-        out_shape=jax.ShapeDtypeStruct((rows, width), bf16),
+        out_shape=pltpu.VMEM((rows, width), bf16),
         in_specs=[hbm] * 11,
         out_specs=vmem,
         scratch_shapes=[

time: 41.8 us -> 39.2 us (0.938)
  Pallas kernels: 40 us -> 38.2 us
  local copies, waits for them, and re-layouts: 1.67 us -> 0.71 us
    pallas_call x1, Pallas kernels: 40 us -> 38.2 us  [local(): pl.pallas_call(functools.partial(kernel, n, heads), out_shape=pltpu.VMEM(...]
    unnamed x1, local copies, waits for them, and re-layouts: 1.67 us -> 0.71 us
where the time goes in v4:
time: 39.2 us; the launch traced here: 38.9 us
  Pallas kernels  38.2 us (97%)
  local copies, waits for them, and re-layouts  0.71 us (2%)
    pallas_call x1, Pallas kernels, local(): pl.pallas_call(functools.partial(kernel, n, heads), out_shape=pltpu.VMEM(...  38.2 us

profile of v4, /device:TPU:2, one launch (start us, length us, event | category | flops | bytes accessed | tf_op | source)
XLA Modules:
  0.0 38.9 jit_solution(5496326616429640156)
XLA Ops:
  0.0 38.2 %shard_map.109 = bf16[256,512]{1,0:T(8,128)(2,1)S(1)} custom-call(bf16[256,512]{1,0:T(8,128)(2,1)} %sig_hbm.1, bf16[256,512]{1,0:T(8,128)(2,1)} %gate_hbm.1, f32[1,512]{1,0:T(1,128)} %bitcast.4, f32[33,64]{1,0:T(8,128)} %wf_hbm.1, f32[1,64]{1,0:T(1,128)} %bitcast.6, f32[1,64]{1,0:T(1,128)} %bitcast.7, f32[64,64]{1,0:T(8,128)} %wm_hbm.1, f32[64,512]{1,0:T(8,128)} %wl_hbm.1, ...), custom_call_target="tpu_custom_call" | custom-call | tf_op jit(solution)/shard_map/pallas_call | solution.py:353
  38.2 0.7 %copy.13 = bf16[256,512]{1,0:T(8,128)(2,1)} copy(bf16[256,512]{1,0:T(8,128)(2,1)S(1)} %shard_map.109) | data formatting | bytes 524288

commit v5 on v3

--- a/solution.py
+++ b/solution.py
@@ -59,15 +59,14 @@
     n, heads, sig_hbm, gate_hbm, skip_hbm, wf_hbm, bf_hbm, freq_hbm, wm_hbm, wl_hbm, rate_hbm, w_hbm, feat_hbm,
     out_ref,
     sig, gate, skip_ref, wf_ref, bf_ref, freq_ref, wm_ref, wl_ref, rate_ref, feat_ref,
-    wc, wrelay, xsend, xrecv, xf, params, h_ref, skips, toep, yf, ysend, yrecv, mixed, part,
-    in_sems, xs_sems, xr_sems, ys_sems, yr_sems, ws_sems, wr_sems, fs_sems, fr_sems, gs_sems, gr_sems,
+    w_own, w_near, xsend, xrecv, xf, params, h_ref, skips, toep, yf, ysend, yrecv, mixed, part, psend, precv,
+    in_sems, xs_sems, xr_sems, ys_sems, yr_sems, ws_sems, wr_sems, fs_sems, fr_sems, gs_sems, gr_sems, ps_sems, pr_sems,
 ):
     me = lax.axis_index("seq")
     hd = lax.axis_index("head")
     rows, width = sig.shape
     group = width // n
     part_group = group // 2
-    chunks = width // LANES
     per_chunk = n // 2
     taps = K // LANES
     blocks = 2 * n
@@ -100,8 +99,9 @@
     load_sig.start()
     for to, _ in everyone:
         pl.semaphore_signal(barrier, inc=1, device_id={"seq": to}, device_id_type=MESH)
-    right, left, opp = lax.rem(hd + 1, heads), lax.rem(hd + heads - 1, heads), lax.rem(hd + 2, heads)
-    for to in (opp, right, left):
+    mate, other = hd + 1 - 2 * lax.rem(hd, 2), heads - 1 - hd
+    opp = lax.rem(hd + 2, heads)
+    for to in (mate, other):
         pl.semaphore_signal(barrier, inc=1, device_id={"head": to}, device_id_type=MESH)
 
     def columns(h):
@@ -110,7 +110,7 @@
     small = (
         (wf_hbm, wf_ref), (bf_hbm, bf_ref), (freq_hbm, freq_ref), (wm_hbm, wm_ref), (wl_hbm, wl_ref),
         (rate_hbm, rate_ref), (skip_hbm, skip_ref), (feat_hbm, feat_ref),
-        (gate_hbm, gate), (w_hbm.at[:, columns(hd)], wc.at[hd]),
+        (gate_hbm, gate), (w_hbm, w_own),
     )
     loads = [pltpu.make_async_copy(src, dst, in_sems.at[i + 1]) for i, (src, dst) in enumerate(small)]
     for load in loads:
@@ -123,7 +123,18 @@
         one, two = swap_halves(piece[:, :, :LANES], piece[:, :, LANES:])
         xsend[h] = jnp.stack([one, two], 1).reshape(n, 8, LANES).astype(jnp.bfloat16)
 
-    pl.semaphore_wait(barrier, n - 1 + heads - 1)
+    pl.semaphore_wait(barrier, n - 1 + 2)
+
+    half = pl.ds(pl.multiple_of(core * (width // 2), width // 2), width // 2)
+    fetches = [
+        pltpu.make_async_remote_copy(
+            src_ref=w_hbm.at[half, columns(of)], dst_ref=w_near.at[i, half], send_sem=ws_sems.at[i],
+            recv_sem=wr_sems.at[i], device_id={"head": to}, device_id_type=MESH,
+        )
+        for i, (of, to) in enumerate(((mate, mate), (opp, mate), (other, other), (opp, other)))
+    ]
+    for i in (0, 2):
+        fetches[i].start()
 
     for h in range(2):
         for to, slot in everyone:
@@ -133,28 +144,6 @@
             ).start()
     for h in range(2):
         xrecv[h, pl.ds(me, 1)] = xsend[h, pl.ds(own_group, 1)]
-
-    half = pl.ds(pl.multiple_of(core * (width // 2), width // 2), width // 2)
-    quarters = [
-        pl.ds(pl.multiple_of(core * (width // 2) + i * (width // 4), width // 4), width // 4) for i in range(2)
-    ]
-
-    def fetch(i, src, dst, to):
-        return pltpu.make_async_remote_copy(
-            src_ref=src, dst_ref=dst, send_sem=ws_sems.at[i], recv_sem=wr_sems.at[i],
-            device_id={"head": to}, device_id_type=MESH,
-        )
-
-    fetches = [
-        fetch(0, w_hbm.at[quarters[0], columns(opp)], wrelay.at[0], right),
-        fetch(1, w_hbm.at[quarters[1], columns(opp)], wrelay.at[1], left),
-        fetch(2, w_hbm.at[half, columns(right)], wc.at[hd, half], right),
-        fetch(3, w_hbm.at[half, columns(left)], wc.at[hd, half], left),
-        fetch(4, wrelay.at[0], wc.at[left, quarters[0]], right),
-        fetch(5, wrelay.at[1], wc.at[right, quarters[1]], left),
-    ]
-    for i in range(4):
-        fetches[i].start()
 
     for load in loads[:8]:
         load.wait()
@@ -207,6 +196,8 @@
         return carry
 
     lax.fori_loop(0, group, build, 0)
+    for i in (1, 3):
+        fetches[i].start()
 
     every = pl.ds(0, n - 1)
     front = taps * part_group
@@ -233,48 +224,38 @@
             yf[h, pl.ds(c, blocks, stride=part_group), :] = conv + rows_of(skips[channel], blocks) * pieces[0]
             return carry
 
-        lax.fori_loop(0, part_group, convolve, 0)
+        lax.fori_loop(0, part_group, convolve, 0, unroll=True)
         ysend[h] = yf[h].reshape(n, 8, LANES).astype(jnp.bfloat16)
-        for to, _ in near + far:
+        for to, _ in far + near:
             pltpu.make_async_remote_copy(
                 src_ref=ysend.at[h, to], dst_ref=yrecv.at[h, own_group], send_sem=ys_sems.at[h],
                 recv_sem=yr_sems.at[h, z_half], device_id={"seq": to}, device_id_type=MESH,
             ).start()
         yrecv[h, pl.ds(own_group, 1)] = ysend[h, pl.ds(me, 1)]
 
-    for i in range(2):
-        fetches[i].wait_recv()
-        fetches[4 + i].start()
-
     def onward(i, ref):
         return pltpu.make_async_remote_copy(
             src_ref=ref, dst_ref=ref, send_sem=fs_sems.at[i], recv_sem=fr_sems.at[i],
             device_id={"seq": partner}, device_id_type=MESH,
         )
 
-    passes = [onward(0, wc.at[left, half]), onward(1, wc.at[right, half]), onward(2, wc.at[opp, half])]
+    passes = [onward(i, w_near.at[i, half]) for i in range(4)]
+    for i in (0, 2):
+        fetches[i].wait_recv()
+        passes[i].start()
     loads[8].wait()
 
-    top, low = pl.ds(0, rows // 2), pl.ds(rows // 2, rows // 2)
-
-    def hop(kind, b, ref, to):
+    sides = (pl.ds(0, rows // 2), pl.ds(rows // 2, rows // 2))
+    neighbours = (mate, other)
+
+    def give(side, b, chunks):
         return pltpu.make_async_remote_copy(
-            src_ref=ref, dst_ref=ref, send_sem=gs_sems.at[kind, b], recv_sem=gr_sems.at[kind, b],
-            device_id={"head": to}, device_id_type=MESH,
+            src_ref=mixed.at[0, chunks, sides[side]], dst_ref=mixed.at[1 + side, chunks, sides[side]],
+            send_sem=gs_sems.at[side, b], recv_sem=gr_sems.at[side, b],
+            device_id={"head": neighbours[side]}, device_id_type=MESH,
         )
 
     order = [(h, z_half if g == 0 else 1 - z_half, g) for h in range(2) for g in range(2)]
-    firsts, seconds = [], []
-
-    def onwards(b):
-        p = order[b][0] * 2 + order[b][1]
-        firsts[b][0].wait_recv()
-        seconds.append(hop(2, b, mixed.at[left, p, top], right))
-        seconds[-1].start()
-        firsts[b][1].wait_recv()
-        seconds.append(hop(3, b, mixed.at[right, p, low], left))
-        seconds[-1].start()
-
     for b, (h, zs, g) in enumerate(order):
         p = h * 2 + zs
         some = pl.ds(0, per_chunk if g else per_chunk - 1)
@@ -285,39 +266,55 @@
         v = yrecv[h, pl.ds(pl.multiple_of(zs * per_chunk, per_chunk), per_chunk)].astype(jnp.float32)
         v = v.reshape(per_chunk // 2, 2, 8, LANES)
         channels = pl.ds(pl.multiple_of(p * LANES, LANES), LANES)
-        for r, piece in enumerate(swap_halves(v[:, 0], v[:, 1])):
-            here = slice(r * LANES, (r + 1) * LANES)
+        for side, piece in enumerate(swap_halves(v[:, 0], v[:, 1])):
+            here = slice(side * LANES, (side + 1) * LANES)
             vt = piece.reshape(LANES, LANES).T
-            mixed[hd, p, here, :] = (gate[here, channels].astype(jnp.float32) * vt).astype(jnp.bfloat16)
-        firsts.append([hop(0, b, mixed.at[hd, p], right), hop(1, b, mixed.at[hd, p], left)])
-        for copy in firsts[b]:
-            copy.start()
-        if b == 1:
-            for i in range(2):
-                fetches[2 + i].wait_recv()
+            mixed[0, p, here, :] = (gate[here, channels].astype(jnp.float32) * vt).astype(jnp.bfloat16)
+        for side in range(2):
+            give(side, h, pl.ds(p, 1)).start()
+        if b == 0:
+            for i in (1, 3):
+                fetches[i].wait_recv()
                 passes[i].start()
-            onwards(0)
-
-    def product(h):
-        lhs = jnp.concatenate([mixed[h, p] for p in range(chunks)], 1)
-        return jnp.dot(lhs, wc[h], preferred_element_type=jnp.float32)
-
-    for i in range(2):
-        fetches[4 + i].wait_recv()
-    passes[2].start()
+
+    def product(slot, side, h, weights, cols):
+        lhs = jnp.concatenate([mixed[slot, 2 * h + i, side * LANES : (side + 1) * LANES] for i in range(2)], 1)
+        depth = slice(h * (width // 2), (h + 1) * (width // 2))
+        return jnp.dot(lhs, weights[depth, cols], preferred_element_type=jnp.float32)
+
+    gifts = [[give(side, h, pl.ds(2 * h, 2)) for h in range(2)] for side in range(2)]
     loads[9].wait()
-    onwards(1)
-    part[...] = product(hd)
-    onwards(2)
-    onwards(3)
     for weights in passes:
         weights.wait_recv()
-    part[...] += product(left) + product(right)
-    for copy in seconds:
-        copy.wait_recv()
-    out_ref[...] = (part[...] + product(opp)).astype(jnp.bfloat16)
-
-    for copies in (*firsts, seconds, passes, fetches):
+    whole = slice(0, width)
+    for side in range(2):
+        gifts[side][0].wait_recv()
+        theirs = columns(neighbours[1 - side])
+        part[side] = (
+            product(0, side, 0, w_own, theirs) + product(0, side, 1, w_own, theirs)
+            + product(1 + side, side, 0, w_near.at[2 * side + 1], whole)
+        )
+    sums = []
+    for side in range(2):
+        gifts[side][1].wait_recv()
+        psend[side] = (part[side] + product(1 + side, side, 1, w_near.at[2 * side + 1], whole)).astype(jnp.bfloat16)
+        sums.append(pltpu.make_async_remote_copy(
+            src_ref=psend.at[side], dst_ref=precv.at[side], send_sem=ps_sems.at[side], recv_sem=pr_sems.at[side],
+            device_id={"head": neighbours[1 - side]}, device_id_type=MESH,
+        ))
+        sums[side].start()
+    for side in range(2):
+        part[side] = sum(
+            product(0, side, h, w_own, columns(hd)) + product(1 + side, side, h, w_near.at[2 * side], whole)
+            for h in range(2)
+        )
+    for side in range(2):
+        sums[side].wait_recv()
+        out_ref[side * LANES : (side + 1) * LANES, :] = (
+            part[side] + precv[side].astype(jnp.float32)
+        ).astype(jnp.bfloat16)
+
+    for copies in (*gifts, sums, passes, fetches):
         for copy in copies:
             copy.wait_send()
     for h in range(2):
@@ -342,7 +339,7 @@
     )
     return pl.pallas_call(
         functools.partial(kernel, n, heads),
-        out_shape=jax.ShapeDtypeStruct((rows, width), bf16),
+        out_shape=pltpu.VMEM((rows, width), bf16),
         in_specs=[hbm] * 11,
         out_specs=vmem,
         scratch_shapes=[
@@ -350,8 +347,8 @@
             pltpu.VMEM((rows, width), bf16),
             *[pltpu.VMEM(a.shape, a.dtype) for a in operands[2:9]],
             pltpu.VMEM(operands[10].shape, f32),
-            pltpu.VMEM((heads, width, width), bf16),
-            pltpu.VMEM((2, width // 4, width), bf16),
+            pltpu.VMEM(out_w.shape, bf16),
+            pltpu.VMEM((4, width, width), bf16),
             pltpu.VMEM((2, n, group, LANES), bf16),
             pltpu.VMEM((2, n, group, LANES), bf16),
             pltpu.VMEM((2, (2 * n + K // LANES) * group // 2, LANES), f32),
@@ -362,10 +359,12 @@
             pltpu.VMEM((2, n * group, LANES), f32),
             pltpu.VMEM((2, n, group, LANES), bf16),
             pltpu.VMEM((2, n, group, LANES), bf16),
-            pltpu.VMEM((heads, width // LANES, rows, LANES), bf16),
-            pltpu.VMEM((rows, width), f32),
-            dma((11,)), dma((2,)), dma((2,)), dma((2,)), dma((2, 2)), dma((6,)), dma((6,)),
-            dma((3,)), dma((3,)), dma((4, width // LANES)), dma((4, width // LANES)),
+            pltpu.VMEM((3, width // LANES, rows, LANES), bf16),
+            pltpu.VMEM((2, rows // 2, width), f32),
+            pltpu.VMEM((2, rows // 2, width), bf16),
+            pltpu.VMEM((2, rows // 2, width), bf16),
+            dma((11,)), dma((2,)), dma((2,)), dma((2,)), dma((2, 2)), dma((4,)), dma((4,)),
+            dma((4,)), dma((4,)), dma((2, 2)), dma((2, 2)), dma((2,)), dma((2,)),
         ],
         compiler_params=pltpu.CompilerParams(collective_id=0, has_side_effects=True),
     )(*operands)

time: 41.8 us -> 37.1 us (0.89)
  Pallas kernels: 40 us -> 35.9 us
  local copies, waits for them, and re-layouts: 1.67 us -> 0.71 us
    pallas_call x1, Pallas kernels: 40 us -> 35.9 us  [local(): pl.pallas_call(functools.partial(kernel, n, heads), out_shape=pltpu.VMEM(...]
    unnamed x1, local copies, waits for them, and re-layouts: 1.67 us -> 0.71 us
where the time goes in v5:
time: 37.1 us; the launch traced here: 36.6 us
  Pallas kernels  35.9 us (97%)
  local copies, waits for them, and re-layouts  0.71 us (2%)
    pallas_call x1, Pallas kernels, local(): pl.pallas_call(functools.partial(kernel, n, heads), out_shape=pltpu.VMEM(...  35.9 us

profile of v5, /device:TPU:2, one launch (start us, length us, event | category | flops | bytes accessed | tf_op | source)
XLA Modules:
  0.0 36.6 jit_solution(7899923667686821597)
XLA Ops:
  0.0 35.9 %shard_map.109 = bf16[256,512]{1,0:T(8,128)(2,1)S(1)} custom-call(bf16[256,512]{1,0:T(8,128)(2,1)} %sig_hbm.1, bf16[256,512]{1,0:T(8,128)(2,1)} %gate_hbm.1, f32[1,512]{1,0:T(1,128)} %bitcast.4, f32[33,64]{1,0:T(8,128)} %wf_hbm.1, f32[1,64]{1,0:T(1,128)} %bitcast.6, f32[1,64]{1,0:T(1,128)} %bitcast.7, f32[64,64]{1,0:T(8,128)} %wm_hbm.1, f32[64,512]{1,0:T(8,128)} %wl_hbm.1, ...), custom_call_target="tpu_custom_call" | custom-call | tf_op jit(solution)/shard_map/pallas_call | solution.py:340
  35.9 0.7 %copy.13 = bf16[256,512]{1,0:T(8,128)(2,1)} copy(bf16[256,512]{1,0:T(8,128)(2,1)S(1)} %shard_map.109) | data formatting | bytes 524288
